TPU v7x, 32 devices: a whole 2x2x4 slice. The times are simulated.
32 devices in a mesh: cg: 8 (over z, x), vg: 4 (over y, core).
Axes of the slice: x: 2, y: 2, z: 4, core: 2. Of those that a mesh axis runs over, the one named last changes fastest.
Arguments:
- con_embed: float32 [32768, 128], P(('cg', 'vg')), may hold values from -6 to 6
- var_embed: float32 [32768, 128], P(('vg', 'cg')), may hold values from -6 to 6
- row_coef: float32 [32768], P(('cg', 'vg')), may hold values from 0.3 to 3
- col_coef: float32 [32768], P(('vg', 'cg')), may hold values from 0.3 to 3
- self_weight: float32 [128, 128], replicated, may hold values from -0.5 to 0.5
- msg_weight: float32 [128, 128], replicated, may hold values from -0.0234375 to 0.0234375
- timestep: int32 [1], replicated, may hold values from 0 to 999
- tile_rows: int32 [8, 4, 16], P('cg', 'vg'), may hold values from 0 to 7, as said below
- tile_cols: int32 [8, 4, 16], P('cg', 'vg'), may hold values from 0 to 15, as said below
- pattern: bfloat16 [8, 4, 16, 512, 512], P('cg', 'vg'), may hold values from -6 to 6
- cotangent: float32 [32768, 128], P(('cg', 'vg')), may hold values from -6 to 6
Outputs:
- con_update: float32 [32768, 128], P(('cg', 'vg'))
- grad_con: float32 [32768, 128], P(('cg', 'vg'))
- grad_var: float32 [32768, 128], P(('vg', 'cg'))
- grad_msg: float32 [128, 128], replicated
- grad_self: float32 [128, 128], replicated
Inputs may be any that keep to these rules, and one draw needn't show every extreme that they name: `tile_rows`: every device lists tile row 0 and tile row 7; a device lists distinct tiles unless 16 exceeds 8 * 16, and repeated tiles add. `tile_cols`: every device lists tile column 0 and tile column 15, together with the rows above: tiles (0, 0) and (7, 15) are on every list.
All inputs are finite; a program needn't handle non-finite values.
Results may differ from a plain program's by a relative error of at most 0.007.
Values may be sent and summed in bfloat16 or wider, within the bound.
A program may use at most 128 MiB of HBM per device.

v0:
```python
import math

import jax
import jax.numpy as jnp
from jax import lax
from jax.sharding import PartitionSpec as P

H = 128
TB = 512


def body(
    con_embed,
    var_embed,
    row_coef,
    col_coef,
    self_weight,
    msg_weight,
    timestep,
    tile_rows,
    tile_cols,
    pattern,
    cotangent,
):
    highest = lax.Precision.HIGHEST
    con_count = con_embed.shape[0]
    var_count = var_embed.shape[0]
    row_blocks = con_count * lax.axis_size("vg") // TB
    col_blocks = var_count * lax.axis_size("cg") // TB
    row_index = tile_rows.reshape(-1)
    col_index = tile_cols.reshape(-1)
    tile_count = row_index.shape[0]
    per_turn = math.gcd(tile_count, 8)
    turns = tile_count // per_turn
    patterns_here = pattern.reshape(turns, per_turn, TB, TB)
    row_turns = row_index.reshape(turns, per_turn)
    col_turns = col_index.reshape(turns, per_turn)
    local_proj = (
        jnp.dot(var_embed, msg_weight, precision=highest, preferred_element_type=jnp.float32)
        * col_coef[:, None]
    ).astype(jnp.bfloat16)
    projected = lax.all_gather(local_proj, "cg", axis=0, tiled=True)
    source_blocks = projected.reshape(col_blocks, TB, H)
    row_ids = jnp.arange(row_blocks, dtype=jnp.int32)
    col_ids = jnp.arange(col_blocks, dtype=jnp.int32)

    def forward_turn(running, inputs):
        rows_now, cols_now, tile_mask = inputs
        products = jnp.einsum(
            "grc,gch->grh", tile_mask, source_blocks[cols_now], preferred_element_type=jnp.float32
        )
        selector = (rows_now[None, :] == row_ids[:, None]).astype(jnp.float32)
        running = running + jnp.dot(
            selector,
            products.reshape(per_turn, TB * H),
            precision=highest,
            preferred_element_type=jnp.float32,
        )
        return (running, None)

    forward_sum, _ = lax.scan(
        forward_turn,
        jnp.zeros((row_blocks, TB * H), jnp.float32),
        (row_turns, col_turns, patterns_here),
    )
    messages = lax.psum_scatter(
        forward_sum.reshape(row_blocks * TB, H), "vg", scatter_dimension=0, tiled=True
    )
    frequency = jnp.exp(-math.log(10000.0) * jnp.arange(H // 2, dtype=jnp.float32) / (H // 2))
    phases = timestep[0].astype(jnp.float32) * frequency
    time_embed = jnp.concatenate([jnp.sin(phases), jnp.cos(phases)])
    preact = (
        jnp.dot(con_embed, self_weight, precision=highest, preferred_element_type=jnp.float32)
        + row_coef[:, None] * messages
        + time_embed[None, :]
    )
    sigmoid_z = jax.nn.sigmoid(preact)
    con_update = con_embed + preact * sigmoid_z
    grad_pre = cotangent * sigmoid_z * (1.0 + preact * (1.0 - sigmoid_z))
    grad_con = cotangent + jnp.dot(
        grad_pre, self_weight.T, precision=highest, preferred_element_type=jnp.float32
    )
    local_self = jnp.dot(
        con_embed.T, grad_pre, precision=highest, preferred_element_type=jnp.float32
    )
    grad_messages = (row_coef[:, None] * grad_pre).astype(jnp.bfloat16)
    whole_rows = lax.all_gather(grad_messages, "vg", axis=0, tiled=True).reshape(row_blocks, TB, H)

    def backward_turn(running, inputs):
        rows_now, cols_now, tile_mask = inputs
        products = jnp.einsum(
            "grc,grh->gch", tile_mask, whole_rows[rows_now], preferred_element_type=jnp.float32
        )
        selector = (cols_now[None, :] == col_ids[:, None]).astype(jnp.float32)
        running = running + jnp.dot(
            selector,
            products.reshape(per_turn, TB * H),
            precision=highest,
            preferred_element_type=jnp.float32,
        )
        return (running, None)

    backward_sum, _ = lax.scan(
        backward_turn,
        jnp.zeros((col_blocks, TB * H), jnp.float32),
        (row_turns, col_turns, patterns_here),
    )
    grad_projected = lax.psum_scatter(
        backward_sum.reshape(col_blocks * TB, H), "cg", scatter_dimension=0, tiled=True
    )
    grad_lin = col_coef[:, None] * grad_projected
    grad_var = jnp.dot(
        grad_lin, msg_weight.T, precision=highest, preferred_element_type=jnp.float32
    )
    local_msg = jnp.dot(
        var_embed.T, grad_lin, precision=highest, preferred_element_type=jnp.float32
    )
    grad_msg, grad_self = lax.psum((local_msg, local_self), ("cg", "vg"))
    return (con_update, grad_con, grad_var, grad_msg, grad_self)


def solution(mesh):
    in_specs = (
        P(("cg", "vg"), None),
        P(("vg", "cg"), None),
        P(("cg", "vg")),
        P(("vg", "cg")),
        P(),
        P(),
        P(),
        P("cg", "vg", None),
        P("cg", "vg", None),
        P("cg", "vg", None, None, None),
        P(("cg", "vg"), None),
    )
    out_specs = (P(("cg", "vg"), None), P(("cg", "vg"), None), P(("vg", "cg"), None), P(), P())
    return jax.shard_map(body, mesh=mesh, in_specs=in_specs, out_specs=out_specs, check_vma=False)
```

profile of v0, /device:TPU:0, one launch (start us, length us, event | category | flops | bytes accessed | tf_op | source)
XLA Modules:
  0.0 396.2 jit_solution(18261910513397852142)
XLA Ops:
  7.2 0.0 all-gather.3.cloned.1.call-start
  7.2 1.0 copy-done
  8.2 2.1 fusion.31
  10.3 0.0 all-gather.3.cloned.1.call-update
  10.3 0.0 reduce-scatter.3.cloned.1.call-start
  10.4 0.5 broadcast.91
  10.9 1.3 reduce.6
  12.2 0.1 reshape_reshape.6
  12.3 1.3 reduce.7
  13.6 0.1 reshape_reshape.7
  13.7 48.8 %all-gather.3.cloned.1.call-done = bf16[8192,128]{1,0:T(8,128)(2,1)} async-done(((bf16[1024,128]{1,0:T(8,128)(2,1)}), bf16[8192,128]{1,0:T(8,128)(2,1)}) %all-gather.3.cloned.1.call-update) | async-done | bytes 2097168 | tf_op jit(solution)/shard_map/all_gather | solution.py:42
  62.5 22.9 %while.22 = (s32[]{:T(128)}, f32[8,65536]{1,0:T(8,128)}, s32[2,8]{1,0:T(2,128)S(1)}, bf16[2,8,512,512]{3,2,1,0:T(8,128)(2,1)}, s32[2,8]{1,0:T(2,128)S(1)}, /*ind...) while((s32[]{:T(128)}, f32[8,65536]{1,0:T(8,128)}, s32[2,8]{1,0:T(2,128)S(1)}, ...), condition=%wide.region_1.2_spmd.clone, body=%wide.region_0.1_spmd.clone.sunk | while | flops 588252224 | bytes 15733575 | solution.py:61
  62.5 3.2 gather_fusion
  65.8 3.7 fusion.65
  69.5 3.6 convolution_add_fusion.6
  73.2 3.2 gather_fusion
  76.4 3.7 fusion.65
  80.2 5.2 %convolution_add_fusion.6 = f32[8,65536]{1,0:T(8,128)} fusion(f32[1,8,512,128]{3,2,1,0:T(8,128)S(1)} %fusion.65, f32[8,65536]{1,0:T(8,128)} %get-tuple-element.252, pred[]{:T(512)S(6)} %compare.6, s32[8]{0:T(128)S(1)} %fusion.66), kind=kOutput, calls=%fused_computation.4.clone.1 | convolution fusion | flops 51380288 | bytes 6291489 | tf_op jit(solution)/shard_map/while/body/eval_jaxpr/dot_general | solution.py:53
  85.4 3.2 reshape.95
  88.6 0.0 reduce-scatter.3.cloned.1.call-update
  88.7 0.0 all-gather.5.cloned.1.call-start
  89.5 0.1 pad_maximum_fusion
  89.6 28.9 %reduce-scatter.3.cloned.1.call-done = f32[1024,128]{1,0:T(8,128)} async-done(((f32[4096,128]{1,0:T(8,128)}), f32[1024,128]{1,0:T(8,128)}) %reduce-scatter.3.cloned.1.call-update) | async-done | bytes 524304 | tf_op jit(solution)/shard_map/reduce_scatter | solution.py:66
  118.5 2.9 multiply_convert_fusion
  121.4 0.0 all-gather.5.cloned.1.call-update
  121.4 0.0 reduce-scatter.5.cloned.1.call-start
  121.5 12.3 %copy.16 = bf16[1,1,16,512,512]{3,4,2,1,0:T(8,128)(2,1)} copy(bf16[1,1,16,512,512]{4,3,2,1,0:T(8,128)(2,1)} %bitcast.88) | data formatting | bytes 16777216 | tf_op args[9]
  133.8 4.5 %all-gather.5.cloned.1.call-done = bf16[4096,128]{1,0:T(8,128)(2,1)} async-done(((bf16[1024,128]{1,0:T(8,128)(2,1)}), bf16[4096,128]{1,0:T(8,128)(2,1)}) %all-gather.5.cloned.1.call-update) | async-done | bytes 1048592 | tf_op jit(solution)/shard_map/all_gather | solution.py:87
  138.3 25.2 %while.23 = (s32[]{:T(128)}, f32[16,65536]{1,0:T(8,128)}, s32[2,8]{1,0:T(2,128)S(1)}, bf16[2,8,512,512]{2,3,1,0:T(8,128)(2,1)}, s32[2,8]{1,0:T(2,128)S(1)}, /*in...) while((s32[]{:T(128)}, f32[16,65536]{1,0:T(8,128)}, s32[2,8]{1,0:T(2,128)S(1)}, ...), condition=%wide.region_4.5_spmd.clone, body=%wide.region_3.4_spmd.clone.sunk | while | flops 639632512 | bytes 19927880 | solution.py:103
  138.3 2.9 gather_fusion.1
  141.2 3.7 fusion.71
  144.9 4.9 %convolution_add_fusion.7 = f32[16,65536]{1,0:T(8,128)} fusion(f32[16,65536]{1,0:T(8,128)} %get-tuple-element.276, f32[1,8,512,128]{3,2,1,0:T(8,128)S(1)} %fusion.71, pred[]{:T(512)S(6)} %compare.7, s32[8]{0:T(128)S(1)} %fusion.72), kind=kOutput, calls=%fused_computation.21.clone.1 | convolution fusion | flops 102760576 | bytes 10485793 | tf_op jit(solution)/shard_map/while/body/eval_jaxpr/dot_general | solution.py:95
  149.8 2.9 gather_fusion.1
  152.7 3.7 fusion.71
  156.5 7.1 %convolution_add_fusion.7 = f32[16,65536]{1,0:T(8,128)} fusion(f32[16,65536]{1,0:T(8,128)} %get-tuple-element.276, f32[1,8,512,128]{3,2,1,0:T(8,128)S(1)} %fusion.71, pred[]{:T(512)S(6)} %compare.7, s32[8]{0:T(128)S(1)} %fusion.72), kind=kOutput, calls=%fused_computation.21.clone.1 | convolution fusion | flops 102760576 | bytes 10485793 | tf_op jit(solution)/shard_map/while/body/eval_jaxpr/dot_general | solution.py:95
  163.5 3.9 reshape.97
  167.4 0.0 reduce-scatter.5.cloned.1.call-update
  167.4 0.2 all-reduce.3.cloned.1.call-start
  167.7 0.8 copy-done.5
  168.4 0.2 copy-done.8
  168.6 1.7 convolution_bitcast_fusion
  170.3 1.5 convolution_add_fusion.2
  171.9 84.1 %reduce-scatter.5.cloned.1.call-done = f32[1024,128]{1,0:T(8,128)} async-done(((f32[8192,128]{1,0:T(8,128)}), f32[1024,128]{1,0:T(8,128)}) %reduce-scatter.5.cloned.1.call-update) | async-done | bytes 524304 | tf_op jit(solution)/shard_map/reduce_scatter | solution.py:108
  256.0 2.8 convolution_bitcast_fusion.1
  258.8 2.5 fusion.33
  261.3 125.3 %all-reduce.3.cloned.1.call-done = (f32[128,128]{0,1:T(8,128)}, f32[128,128]{0,1:T(8,128)}) async-done(((f32[128,128]{0,1:T(8,128)}, f32[128,128]{0,1:T(8,128)}), (f32[128,128]{0,1:T(8,128)}, f32[128,128]{0,1:T(8,128)})) %all-reduce.3.cloned.1.call-update) | async-done | bytes 131088 | tf_op jit(solution)/shard_map/psum | solution.py:118
  386.6 1.6 copy.18
  388.1 1.6 copy.19
  (31 shorter events, 0.2 us)
Async XLA Ops:
  7.2 1.0 copy-start
  7.2 55.3 %all-gather.3.cloned.1.call-start = ((), (), s32[]{:S(2)}) async-start(), calls=%async_computation.2 | async-start | bytes 2359296 | tf_op jit(solution)/shard_map/all_gather | solution.py:42
  10.3 108.2 %reduce-scatter.3.cloned.1.call-start = ((), (), s32[]{:S(2)}) async-start(), calls=%async_computation.3 | async-start | bytes 2621440 | tf_op jit(solution)/shard_map/reduce_scatter | solution.py:66
  88.6 29.9 %copy-start.3 = (f32[1024,128]{1,0:T(8,128)S(1)}, f32[1024,128]{1,0:T(8,128)}, u32[]{:S(2)}) copy-start(f32[1024,128]{1,0:T(8,128)} %param.15) | copy-start | bytes 1572868
  88.6 29.9 %copy-start.4 = (f32[1024,128]{1,0:T(8,128)S(1)}, f32[1024,128]{1,0:T(8,128)}, u32[]{:S(2)}) copy-start(f32[1024,128]{1,0:T(8,128)} %param.25) | copy-start | bytes 1572868
  88.6 29.9 %copy-start.6 = (f32[128,128]{1,0:T(8,128)S(1)}, f32[128,128]{1,0:T(8,128)}, u32[]{:S(2)}) copy-start(f32[128,128]{1,0:T(8,128)} %param.19) | copy-start | bytes 196612
  88.6 29.9 %copy-start.7 = (f32[1024]{0:T(1024)S(1)}, f32[1024]{0:T(1024)}, u32[]{:S(2)}) copy-start(f32[1024]{0:T(1024)} %param.17) | copy-start | bytes 12292
  88.7 49.6 %all-gather.5.cloned.1.call-start = ((), (), s32[]{:S(2)}) async-start(), calls=%async_computation.4 | async-start | bytes 1310720 | tf_op jit(solution)/shard_map/all_gather | solution.py:87
  121.4 134.5 %reduce-scatter.5.cloned.1.call-start = ((), (), s32[]{:S(2)}) async-start(), calls=%async_computation.5 | async-start | bytes 4718592 | tf_op jit(solution)/shard_map/reduce_scatter | solution.py:108
  167.4 1.0 copy-start.5
  167.4 1.2 copy-start.8
  167.4 219.2 %all-reduce.3.cloned.1.call-start = ((), (), s32[]{:S(2)}) async-start(), calls=%async_computation.6 | async-start | bytes 262144 | tf_op jit(solution)/shard_map/psum | solution.py:118
  170.3 85.6 %copy-start.2 = (f32[1024]{0:T(1024)S(1)}, f32[1024]{0:T(1024)}, u32[]{:S(2)}) copy-start(f32[1024]{0:T(1024)} %param.18) | copy-start | bytes 12292
  170.3 88.5 %copy-start.1 = (f32[128,128]{1,0:T(8,128)S(1)}, f32[128,128]{1,0:T(8,128)}, u32[]{:S(2)}) copy-start(f32[128,128]{1,0:T(8,128)} %param.20) | copy-start | bytes 196612
Sparse Core Ops, SparseCore 0:
  10.7 51.7 all-gather.2
  88.8 29.6 reduce-scatter.2
  121.5 16.7 all-gather.4
  167.5 88.3 reduce-scatter.4
  262.1 124.4 all-reduce.2
where the time goes:
time: 397 us; the launch traced here: 396 us
  waiting for transfers between devices  292 us (74%)
  matrix products  49.2 us (12%)
  local copies, waits for them, and re-layouts  37.4 us (9%)
  between operations  14.6 us (4%)
    psum x1, waiting for transfers between devices, body(): grad_msg, grad_self = lax.psum((local_msg, local_self), ('cg', 'vg'))  125 us
    reduce_scatter x1, waiting for transfers between devices, body(): lax.psum_scatter(backward_sum.reshape(col_blocks * TB, H), 'cg', scatter_...  84.1 us
    all_gather x1, waiting for transfers between devices, body(): projected = lax.all_gather(local_proj, 'cg', axis=0, tiled=True)  48.8 us
    reduce_scatter x1, waiting for transfers between devices, body(): lax.psum_scatter(forward_sum.reshape(row_blocks * TB, H), 'vg', scatter_d...  28.9 us
    unnamed x22, local copies, waits for them, and re-layouts  17.9 us
    dot_general x2, matrix products, backward_turn(): jnp.dot(selector, products.reshape(per_turn, TB * H), precision=highest,...  12 us
    dot_general x2, matrix products, forward_turn(): jnp.dot(selector, products.reshape(per_turn, TB * H), precision=highest,...  8.83 us
  transfers between devices with their start and end apart: 5, of which 5 were waited for; matrix products, arithmetic and copies ran while one was open for 5% of the time, Pallas kernels for 0%

commit v1 on v0

v1 whole, which is shorter than its diff:
```python
import functools
import math

import jax
import jax.numpy as jnp
from jax import lax
from jax.experimental import pallas as pl
from jax.experimental.pallas import tpu as pltpu
from jax.sharding import PartitionSpec as P

H = 128
TB = 512
CHUNKS = 4
MESH = pl.DeviceIdType.MESH
HIGHEST = lax.Precision.HIGHEST
F32 = jnp.float32
BF16 = jnp.bfloat16


def rcopy(src, dst, send_sem, recv_sem, device):
    return pltpu.make_async_remote_copy(
        src_ref=src, dst_ref=dst, send_sem=send_sem, recv_sem=recv_sem,
        device_id=device, device_id_type=MESH,
    )


def rows(index, size):
    return pl.ds(pl.multiple_of(index * size, size), size)


def dot(a, b, dims=((1,), (0,))):
    return lax.dot_general(a, b, (dims, ((), ())), precision=HIGHEST, preferred_element_type=F32)


def column(coef_ref, out_ref):
    for i in range(coef_ref.shape[0]):
        out_ref[pl.ds(i * H, H), :] = jnp.broadcast_to(coef_ref[pl.ds(i, 1), :], (H, H)).T


def gather_kernel(n_cg, var_ref, weight_ref, coef_ref, out_ref, coef, send, recv_z, recv_x):
    n_z = n_cg // 2
    cg, vg = lax.axis_index("cg"), lax.axis_index("vg")
    z, x = cg // 2, cg % 2
    size = var_ref.shape[0]
    barrier = pltpu.get_barrier_semaphore()
    pl.semaphore_signal(barrier, inc=1, device_id=(z * 2 + 1 - x, vg), device_id_type=MESH)
    for s in (1, -1):
        @pl.when((z + s >= 0) & (z + s < n_z))
        def _():
            pl.semaphore_signal(barrier, inc=1, device_id=((z + s) * 2 + x, vg), device_id_type=MESH)

    column(coef_ref, coef)
    out_ref[rows(cg, size), :] = (dot(var_ref[...], weight_ref[...]) * coef[...]).astype(BF16)
    lines = jnp.where(z > 0, 1, 0) + jnp.where(z < n_z - 1, 1, 0)
    pl.semaphore_wait(barrier, 1 + lines)

    def z_copy(zs, way):
        block = out_ref.at[rows(zs * 2 + x, size), :]
        step = 1 if way == 0 else -1
        return rcopy(block, block, send.at[way, zs], recv_z.at[zs], ((z + step) * 2 + x, vg))

    def x_copy(zs):
        block = out_ref.at[rows(zs * 2 + x, size), :]
        return rcopy(block, block, send.at[2, zs], recv_x.at[zs], (z * 2 + 1 - x, vg))

    def x_wait(zs):
        block = out_ref.at[rows(zs * 2 + 1 - x, size), :]
        rcopy(block, block, send.at[2, zs], recv_x.at[zs], (z * 2 + 1 - x, vg)).wait_recv()

    def on(zs, way, act):
        if way == 0:
            pl.when((zs >= 0) & (zs <= z) & (z + 1 < n_z))(act)
        else:
            pl.when((zs < n_z) & (zs >= z) & (z >= 1))(act)

    for way in (0, 1):
        on(z, way, lambda way=way: z_copy(z, way).start())
    x_copy(z).start()
    for d in range(1, n_z):
        for way in (0, 1):
            zs = z - d if way == 0 else z + d

            @pl.when((zs >= 0) & (zs < n_z))
            def _(zs=zs, way=way):
                z_copy(zs, way).wait_recv()
                on(zs, way, lambda: z_copy(zs, way).start())
                x_copy(zs).start()

    for zs in range(n_z):
        x_wait(zs)
        x_copy(zs).wait_send()
    for d in range(n_z):
        for way in (0, 1):
            zs = z - d if way == 0 else z + d
            on(zs, way, lambda zs=zs, way=way: z_copy(zs, way).wait_send())


def gather_projected(var_embed, msg_weight, col_coef, n_cg):
    size = var_embed.shape[0]
    vmem = pl.BlockSpec(memory_space=pltpu.VMEM)
    return pl.pallas_call(
        functools.partial(gather_kernel, n_cg),
        name="gather_projected",
        out_shape=jax.ShapeDtypeStruct((n_cg * size, H), BF16),
        in_specs=[vmem] * 3,
        out_specs=vmem,
        scratch_shapes=[
            pltpu.VMEM((size, H), F32),
            pltpu.SemaphoreType.DMA((3, n_cg // 2)),
            pltpu.SemaphoreType.DMA((n_cg // 2,)),
            pltpu.SemaphoreType.DMA((n_cg // 2,)),
        ],
        compiler_params=pltpu.CompilerParams(collective_id=0, has_side_effects=True),
    )(var_embed, msg_weight, col_coef.reshape(-1, H))


def tile_kernel(per, transposed, to_ref, from_ref, pattern_ref, source_ref, out_ref):
    step = pl.program_id(0)

    @pl.when(step == 0)
    def _():
        out_ref[...] = jnp.zeros_like(out_ref)

    for t in range(per):
        k = step * per + t
        source = source_ref[rows(from_ref[k], TB), :]
        dims = ((0,), (0,)) if transposed else ((1,), (0,))
        target = rows(to_ref[k], TB)
        out_ref[target, :] += lax.dot_general(
            pattern_ref[t], source, (dims, ((), ())), preferred_element_type=F32
        )


def tile_sum(to_index, from_index, patterns, source, out_rows, transposed):
    count = patterns.shape[0]
    per = math.gcd(count, 4)
    return pl.pallas_call(
        functools.partial(tile_kernel, per, transposed),
        name="tiles_back" if transposed else "tiles_forward",
        out_shape=jax.ShapeDtypeStruct((out_rows, H), F32),
        grid_spec=pltpu.PrefetchScalarGridSpec(
            num_scalar_prefetch=2,
            grid=(count // per,),
            in_specs=[
                pl.BlockSpec((per, TB, TB), lambda i, *_: (i, 0, 0)),
                pl.BlockSpec(source.shape, lambda i, *_: (0, 0)),
            ],
            out_specs=pl.BlockSpec((out_rows, H), lambda i, *_: (0, 0)),
        ),
        compiler_params=pltpu.CompilerParams(dimension_semantics=("arbitrary",)),
    )(to_index, from_index, patterns, source)


def middle_kernel(
    n_vg, part_ref, con_ref, cot_ref, weight_ref, coef_ref, time_ref,
    update_ref, grad_con_ref, self_ref, whole_ref,
    coef, pre, from_core, to_peer, from_peer,
    core_send, core_recv, peer_send, peer_recv, own_send, pass_send, block_recv, pair_recv,
):
    n_hi = n_vg // 2
    cg, vg = lax.axis_index("cg"), lax.axis_index("vg")
    hi, core = vg // 2, vg % 2
    pair = (cg, hi * 2 + 1 - core)
    size = con_ref.shape[0]
    piece = size // CHUNKS
    barrier = pltpu.get_barrier_semaphore()
    pl.semaphore_signal(barrier, inc=1, device_id=pair, device_id_type=MESH)
    ups = [lax.rem(hi + j, n_hi) for j in range(n_hi)]
    downs = [lax.rem(hi + n_hi - j, n_hi) for j in range(n_hi)]
    for j in range(1, n_hi):
        pl.semaphore_signal(barrier, inc=1, device_id=(cg, ups[j] * 2 + core), device_id_type=MESH)
    pl.semaphore_wait(barrier, n_hi)

    def cut(block, k):
        return rows(block * CHUNKS + k, piece)

    def core_copy(h, k):
        return rcopy(
            part_ref.at[cut(h * 2 + 1 - core, k), :], from_core.at[cut(h, k), :],
            core_send.at[h, k], core_recv.at[h, k], pair,
        )

    def peer_copy(j, k):
        return rcopy(
            to_peer.at[cut(j - 1, k), :], from_peer.at[cut(j - 1, k), :],
            peer_send.at[j - 1, k], peer_recv.at[j - 1, k], (cg, ups[j] * 2 + core),
        )

    def own_copy(j, k):
        block = whole_ref.at[cut(vg, k), :]
        return rcopy(block, block, own_send.at[j - 1, k], block_recv.at[j - 1, k], (cg, ups[j] * 2 + core))

    def block_wait(j, k):
        block = whole_ref.at[cut(downs[j] * 2 + core, k), :]
        rcopy(block, block, own_send.at[j - 1, k], block_recv.at[j - 1, k], pair).wait_recv()

    def pass_copy(h, k):
        block = whole_ref.at[cut(h * 2 + core, k), :]
        return rcopy(block, block, pass_send.at[h, k], pair_recv.at[h, k], pair)

    def pass_wait(h, k):
        block = whole_ref.at[cut(h * 2 + 1 - core, k), :]
        rcopy(block, block, pass_send.at[h, k], pair_recv.at[h, k], pair).wait_recv()

    for j in list(range(1, n_hi)) + [0]:
        for k in range(CHUNKS):
            core_copy(ups[j], k).start()
    for j in range(1, n_hi):
        for k in range(CHUNKS):
            core_copy(ups[j], k).wait_recv()
            to_peer[cut(j - 1, k), :] = (
                part_ref[cut(ups[j] * 2 + core, k), :] + from_core[cut(ups[j], k), :]
            ).astype(BF16)
            peer_copy(j, k).start()
    column(coef_ref, coef)
    pre[...] = dot(con_ref[...], weight_ref[...]) + time_ref[...]
    for k in range(CHUNKS):
        core_copy(hi, k).wait_recv()
        here = pl.ds(k * piece, piece)
        messages = part_ref[cut(vg, k), :] + from_core[cut(hi, k), :]
        for j in range(1, n_hi):
            peer_copy(j, k).wait_recv()
            messages = messages + from_peer[cut(j - 1, k), :].astype(F32)
        preact = pre[here, :] + coef[here, :] * messages
        sig = jax.nn.sigmoid(preact)
        update_ref[here, :] = con_ref[here, :] + preact * sig
        grad_pre = cot_ref[here, :] * sig * (1.0 + preact * (1.0 - sig))
        pre[here, :] = grad_pre
        whole_ref[cut(vg, k), :] = (coef[here, :] * grad_pre).astype(BF16)
        for j in range(1, n_hi):
            own_copy(j, k).start()
        pass_copy(hi, k).start()
    grad_con_ref[...] = cot_ref[...] + dot(pre[...], weight_ref[...], ((1,), (1,)))
    self_ref[...] = dot(con_ref[...], pre[...], ((0,), (0,)))
    for k in range(CHUNKS):
        for j in range(1, n_hi):
            block_wait(j, k)
            pass_copy(downs[j], k).start()
    for h in range(n_hi):
        for k in range(CHUNKS):
            pass_wait(h, k)
            pass_copy(h, k).wait_send()
            core_copy(h, k).wait_send()
    for j in range(1, n_hi):
        for k in range(CHUNKS):
            peer_copy(j, k).wait_send()
            own_copy(j, k).wait_send()


def middle(part, con_embed, cotangent, self_weight, row_coef, time_embed, n_vg):
    size = con_embed.shape[0]
    n_hi = n_vg // 2
    vmem = pl.BlockSpec(memory_space=pltpu.VMEM)
    full = jax.ShapeDtypeStruct((size, H), F32)
    others = max(n_hi - 1, 1)
    dma = lambda n: pltpu.SemaphoreType.DMA((n, CHUNKS))
    return pl.pallas_call(
        functools.partial(middle_kernel, n_vg),
        name="middle",
        out_shape=(
            full, full, jax.ShapeDtypeStruct((H, H), F32),
            jax.ShapeDtypeStruct((n_vg * size, H), BF16),
        ),
        in_specs=[vmem] * 6,
        out_specs=(vmem,) * 4,
        scratch_shapes=[
            pltpu.VMEM((size, H), F32),
            pltpu.VMEM((size, H), F32),
            pltpu.VMEM((n_hi * size, H), F32),
            pltpu.VMEM((others * size, H), BF16),
            pltpu.VMEM((others * size, H), BF16),
            dma(n_hi), dma(n_hi), dma(others), dma(others),
            dma(others), dma(n_hi), dma(others), dma(n_hi),
        ],
        compiler_params=pltpu.CompilerParams(collective_id=1, has_side_effects=True),
    )(part, con_embed, cotangent, self_weight, row_coef.reshape(-1, H), time_embed.reshape(1, H))


class Total:
    def __init__(self, n_cg, n_vg, local, out, cuts, quarters, sem):
        self.n_cg, self.n_vg = n_cg, n_vg
        self.local, self.out, self.cuts, self.quarters, self.sem = local, out, cuts, quarters, sem
        self.cg, self.vg = lax.axis_index("cg"), lax.axis_index("vg")
        self.size = H // n_vg

    def a(self, j):
        v = lax.rem(self.vg + j, self.n_vg)
        return rcopy(
            self.local.at[rows(v, self.size), :], self.cuts.at[j - 1],
            self.sem.at[0, j], self.sem.at[1, j], (self.cg, v),
        )

    def b(self, j):
        c = lax.rem(self.cg + j, self.n_cg)
        block = self.quarters.at[self.cg]
        return rcopy(block, block, self.sem.at[2, j], self.sem.at[3, j], (c, self.vg))

    def b_wait(self, j):
        c = lax.rem(self.cg + self.n_cg - j, self.n_cg)
        block = self.quarters.at[c]
        rcopy(block, block, self.sem.at[2, j], self.sem.at[3, j], (c, self.vg)).wait_recv()

    def c(self, j):
        v = lax.rem(self.vg + j, self.n_vg)
        block = self.out.at[rows(self.vg, self.size), :]
        return rcopy(block, block, self.sem.at[4, j], self.sem.at[5, j], (self.cg, v))

    def c_wait(self, j):
        v = lax.rem(self.vg + self.n_vg - j, self.n_vg)
        block = self.out.at[rows(v, self.size), :]
        rcopy(block, block, self.sem.at[4, j], self.sem.at[5, j], (self.cg, v)).wait_recv()

    def start(self):
        for j in range(1, self.n_vg):
            self.a(j).start()

    def second(self):
        value = self.local[rows(self.vg, self.size), :]
        for j in range(1, self.n_vg):
            self.a(j).wait_recv()
            value = value + self.cuts[j - 1]
        self.quarters[self.cg] = value
        for j in range(1, self.n_cg):
            self.b(j).start()

    def third(self):
        for j in range(1, self.n_cg):
            self.b_wait(j)
            self.b(j).wait_send()
        value = self.quarters[0]
        for c in range(1, self.n_cg):
            value = value + self.quarters[c]
        self.out[rows(self.vg, self.size), :] = value
        for j in range(1, self.n_vg):
            self.c(j).start()

    def finish(self):
        for j in range(1, self.n_vg):
            self.c_wait(j)
            self.c(j).wait_send()
            self.a(j).wait_send()


def last_kernel(
    n_cg, n_vg, part_ref, var_ref, weight_ref, coef_ref, self_ref,
    grad_var_ref, grad_msg_ref, grad_self_ref,
    coef, to_x, from_x, to_z, from_z, local_msg,
    cuts_a, cuts_b, quarters_a, quarters_b, x_send, x_recv, z_send, z_recv, sem_a, sem_b,
):
    n_z = n_cg // 2
    cg, vg = lax.axis_index("cg"), lax.axis_index("vg")
    z, x = cg // 2, cg % 2
    size = var_ref.shape[0]
    barrier = pltpu.get_barrier_semaphore()
    for j in range(1, n_cg):
        pl.semaphore_signal(barrier, inc=1, device_id=(lax.rem(cg + j, n_cg), vg), device_id_type=MESH)
    for j in range(1, n_vg):
        pl.semaphore_signal(barrier, inc=1, device_id=(cg, lax.rem(vg + j, n_vg)), device_id_type=MESH)
    pl.semaphore_wait(barrier, n_cg + n_vg - 2)

    def x_copy(zd):
        return rcopy(to_x.at[zd], from_x.at[zd], x_send.at[zd], x_recv.at[zd], (z * 2 + 1 - x, vg))

    def z_copy(zd, way):
        step = 1 if way == 0 else -1
        return rcopy(
            to_z.at[zd], from_z.at[way, zd], z_send.at[way, zd], z_recv.at[way, zd], ((z + step) * 2 + x, vg)
        )

    def z_arrives(way):
        return z >= 1 if way == 0 else z + 1 < n_z

    order = [(d, way) for d in range(n_z - 1, 0, -1) for way in (0, 1)]

    def place(d, way):
        zd = z + d if way == 0 else z - d
        return zd, (zd >= 0) & (zd < n_z)

    def send_x(zd):
        to_x[zd] = part_ref[rows(zd * 2 + 1 - x, size), :].astype(BF16)
        x_copy(zd).start()

    for d, way in order:
        zd, there = place(d, way)
        pl.when(there)(lambda zd=zd: send_x(zd))
    send_x(z)
    small = Total(n_cg, n_vg, self_ref, grad_self_ref, cuts_a, quarters_a, sem_a)
    small.start()
    column(coef_ref, coef)
    small.second()

    for d, way in order:
        zd, there = place(d, way)

        @pl.when(there)
        def _(zd=zd, way=way):
            x_copy(zd).wait_recv()
            here = part_ref[rows(zd * 2 + x, size), :] + from_x[zd].astype(F32)

            @pl.when(z_arrives(way))
            def _():
                z_copy(zd, way).wait_recv()
                to_z[zd] = (here + from_z[way, zd].astype(F32)).astype(BF16)

            @pl.when(jnp.logical_not(z_arrives(way)))
            def _():
                to_z[zd] = here.astype(BF16)

            z_copy(zd, way).start()

    small.third()
    x_copy(z).wait_recv()
    coef_now = coef[...]
    grad_var_ref[...] = part_ref[rows(cg, size), :] + from_x[z].astype(F32)
    for way in (0, 1):
        @pl.when(z_arrives(way))
        def _(way=way):
            z_copy(z, way).wait_recv()
            grad_var_ref[...] += from_z[way, z].astype(F32)

    coef[...] = grad_var_ref[...] * coef_now
    local_msg[...] = dot(var_ref[...], coef[...], ((0,), (0,)))
    big = Total(n_cg, n_vg, local_msg, grad_msg_ref, cuts_b, quarters_b, sem_b)
    big.start()
    grad_var_ref[...] = dot(coef[...], weight_ref[...], ((1,), (1,)))
    big.second()
    for d, way in order:
        zd, there = place(d, way)
        pl.when(there)(lambda zd=zd, way=way: z_copy(zd, way).wait_send())
    for zd in range(n_z):
        x_copy(zd).wait_send()
    small.finish()
    big.third()
    big.finish()


def last(part, var_embed, msg_weight, col_coef, local_self, n_cg, n_vg):
    size = var_embed.shape[0]
    n_z = n_cg // 2
    n_max = max(n_cg, n_vg)
    cut = H // n_vg
    vmem = pl.BlockSpec(memory_space=pltpu.VMEM)
    square = jax.ShapeDtypeStruct((H, H), F32)
    return pl.pallas_call(
        functools.partial(last_kernel, n_cg, n_vg),
        name="last",
        out_shape=(jax.ShapeDtypeStruct((size, H), F32), square, square),
        in_specs=[vmem] * 5,
        out_specs=(vmem,) * 3,
        scratch_shapes=[
            pltpu.VMEM((size, H), F32),
            pltpu.VMEM((n_z, size, H), BF16),
            pltpu.VMEM((n_z, size, H), BF16),
            pltpu.VMEM((n_z, size, H), BF16),
            pltpu.VMEM((2, n_z, size, H), BF16),
            pltpu.VMEM((H, H), F32),
            pltpu.VMEM((n_vg - 1, cut, H), F32),
            pltpu.VMEM((n_vg - 1, cut, H), F32),
            pltpu.VMEM((n_cg, cut, H), F32),
            pltpu.VMEM((n_cg, cut, H), F32),
            pltpu.SemaphoreType.DMA((n_z,)),
            pltpu.SemaphoreType.DMA((n_z,)),
            pltpu.SemaphoreType.DMA((2, n_z)),
            pltpu.SemaphoreType.DMA((2, n_z)),
            pltpu.SemaphoreType.DMA((6, n_max)),
            pltpu.SemaphoreType.DMA((6, n_max)),
        ],
        compiler_params=pltpu.CompilerParams(collective_id=2, has_side_effects=True),
    )(part, var_embed, msg_weight, col_coef.reshape(-1, H), local_self)


def body(
    con_embed, var_embed, row_coef, col_coef, self_weight, msg_weight,
    timestep, tile_rows, tile_cols, pattern, cotangent,
):
    n_cg, n_vg = lax.axis_size("cg"), lax.axis_size("vg")
    group_rows = con_embed.shape[0] * n_vg
    group_cols = var_embed.shape[0] * n_cg
    row_index = tile_rows.reshape(-1)
    col_index = tile_cols.reshape(-1)
    patterns = pattern.reshape(-1, TB, TB)
    frequency = jnp.exp(-math.log(10000.0) * jnp.arange(H // 2, dtype=F32) / (H // 2))
    phases = timestep[0].astype(F32) * frequency
    time_embed = jnp.concatenate([jnp.sin(phases), jnp.cos(phases)])

    projected = gather_projected(var_embed, msg_weight, col_coef, n_cg)
    forward_sum = tile_sum(row_index, col_index, patterns, projected, group_rows, False)
    con_update, grad_con, local_self, whole_rows = middle(
        forward_sum, con_embed, cotangent, self_weight, row_coef, time_embed, n_vg
    )
    backward_sum = tile_sum(col_index, row_index, patterns, whole_rows, group_cols, True)
    grad_var, grad_msg, grad_self = last(
        backward_sum, var_embed, msg_weight, col_coef, local_self, n_cg, n_vg
    )
    return (con_update, grad_con, grad_var, grad_msg, grad_self)


def solution(mesh):
    in_specs = (
        P(("cg", "vg"), None),
        P(("vg", "cg"), None),
        P(("cg", "vg")),
        P(("vg", "cg")),
        P(),
        P(),
        P(),
        P("cg", "vg", None),
        P("cg", "vg", None),
        P("cg", "vg", None, None, None),
        P(("cg", "vg"), None),
    )
    out_specs = (P(("cg", "vg"), None), P(("cg", "vg"), None), P(("vg", "cg"), None), P(), P())
    return jax.shard_map(body, mesh=mesh, in_specs=in_specs, out_specs=out_specs, check_vma=False)
```

time: 397 us -> 122 us (0.31)
  waiting for transfers between devices: 292 us -> 0 us
  Pallas kernels: 0 us -> 114 us
  matrix products: 49.2 us -> 0 us
  local copies, waits for them, and re-layouts: 37.4 us -> 6.41 us
  between operations: 14.6 us -> 1.32 us
    psum x1 -> x0, waiting for transfers between devices: 125 us -> none  [body(): grad_msg, grad_self = lax.psum((local_msg, local_self), ('cg', 'vg'))]
    pallas_call x0 -> x5, Pallas kernels: none -> 114 us  [the longest x1 44 us: last(): pl.pallas_call(functools.partial(last_kernel, n_cg, n_vg), name='last', o...]
    reduce_scatter x2 -> x0, waiting for transfers between devices: 113 us -> none  [the longest x1 84.1 us: body(): lax.psum_scatter(backward_sum.reshape(col_blocks * TB, H), 'cg', scatter_...]
    all_gather x2 -> x0, waiting for transfers between devices: 53.3 us -> none  [the longest x1 48.8 us: body(): projected = lax.all_gather(local_proj, 'cg', axis=0, tiled=True)]
    dot_general x14 -> x0, matrix products: 49.2 us -> none  [the longest x2 12 us: backward_turn(): jnp.dot(selector, products.reshape(per_turn, TB * H), precision=highest,...]
    gather x4 -> x0, local copies, waits for them, and re-layouts: 12.2 us -> none  [the longest x2 6.48 us: forward_turn(): source_blocks[cols_now]]
    unnamed x22 -> x9, local copies, waits for them, and re-layouts: 17.9 us -> 6.41 us
    reshape x2 -> x0, local copies, waits for them, and re-layouts: 7.09 us -> none  [the longest x1 3.86 us: body(): backward_sum.reshape(col_blocks * TB, H)]
  transfers between devices with their start and end apart: 5 -> 0, of which waited for: 5 -> 0; matrix products, arithmetic and copies ran while one was open for 5% -> 0% of each run, Pallas kernels for 0% -> 0%
where the time goes in v1:
time: 122 us
  Pallas kernels  114 us (93%)
  local copies, waits for them, and re-layouts  6.41 us (5%)
  between operations  1.32 us (1%)
    pallas_call x1, Pallas kernels, last(): pl.pallas_call(functools.partial(last_kernel, n_cg, n_vg), name='last', o...  44 us
    pallas_call x1, Pallas kernels, gather_projected(): pl.pallas_call(functools.partial(gather_kernel, n_cg), name='gather_proje...  32.6 us
    pallas_call x1, Pallas kernels, middle(): pl.pallas_call(functools.partial(middle_kernel, n_vg), name='middle', out...  20 us
    pallas_call x2, Pallas kernels, tile_sum(): pl.pallas_call(functools.partial(tile_kernel, per, transposed), name='til...  17.1 us
    unnamed x9, local copies, waits for them, and re-layouts  6.41 us

profile of v1, /device:TPU:0, one launch (start us, length us, event | category | flops | bytes accessed | tf_op | source)
XLA Modules:
  0.0 122.0 jit_solution(8633294221950553503)
XLA Ops:
  1.3 0.6 maximum_bitcast_fusion.time_ref
  1.9 32.6 %gather_projected.1.source_ref = bf16[8192,128]{1,0:T(8,128)(2,1)} custom-call(f32[1024,128]{1,0:T(8,128)} %var_ref.3, f32[128,128]{1,0:T(8,128)} %weight_ref.5, f32[8,128]{1,0:T(8,128)} %bitcast.10), custom_call_target="tpu_custom_call" | custom-call | tf_op jit(solution)/shard_map/gather_projected/pallas_call | solution.py:101
  34.5 8.3 %tiles_forward.1.part_ref = f32[4096,128]{1,0:T(8,128)} custom-call(s32[16]{0:T(128)} %bitcast.13, s32[16]{0:T(128)} %bitcast.15, bf16[16,512,512]{2,1,0:T(8,128)(2,1)} %bitcast.8, bf16[8192,128]{1,0:T(8,128)(2,1)} %gather_projected.1.source_ref), custom_call_target="tpu_custom_call" | custom-call | tf_op jit(solution)/shard_map/tiles_forward/pallas_call | solution.py:137
  42.8 20.0 %middle.1 = (f32[1024,128]{1,0:T(8,128)}, f32[1024,128]{1,0:T(8,128)}, f32[128,128]{1,0:T(8,128)}, bf16[4096,128]{1,0:T(8,128)(2,1)}) custom-call(f32[4096,128]{1,0:T(8,128)} %tiles_forward.1.part_ref, f32[1024,128]{1,0:T(8,128)} %con_ref.1, f32[1024,128]{1,0:T(8,128)} %cot_ref.1, f32[128,128]{1,0:T(8,128)} %weight_ref.4, f32[8,128]{1,0:T(8,128)} %bitcast.12, ...), custom_call_target="tpu_custom_call" | custom-call | tf_op jit(solution)/shard_map/middle/pallas_call | solution.py:257
  62.8 8.8 %tiles_back.1.part_ref = f32[8192,128]{1,0:T(8,128)} custom-call(s32[16]{0:T(128)} %bitcast.16, s32[16]{0:T(128)} %bitcast.14, bf16[16,512,512]{2,1,0:T(8,128)(2,1)} %bitcast.9, bf16[4096,128]{1,0:T(8,128)(2,1)} %get-tuple-element.14.source_ref), custom_call_target="tpu_custom_call" | custom-call | tf_op jit(solution)/shard_map/tiles_back/pallas_call | solution.py:137
  71.6 0.0 copy-start.1
  71.6 0.0 copy-start
  71.6 44.0 %last.1 = (f32[1024,128]{1,0:T(8,128)}, f32[128,128]{1,0:T(8,128)}, f32[128,128]{1,0:T(8,128)}) custom-call(f32[8192,128]{1,0:T(8,128)} %tiles_back.1.part_ref, f32[1024,128]{1,0:T(8,128)} %var_ref.3, f32[128,128]{1,0:T(8,128)} %weight_ref.5, f32[8,128]{1,0:T(8,128)} %bitcast.11, f32[128,128]{1,0:T(8,128)} %get-tuple-element.15.self_ref), custom_call_target="tpu_custom_call" | custom-call | tf_op jit(solution)/shard_map/last/pallas_call | solution.py:444
  115.6 0.0 copy-done.1
  115.6 0.8 copy.22
  116.4 0.0 copy-done
  116.4 0.8 copy.23
  117.2 1.9 %copy.24 = f32[1024,128]{1,0:T(8,128)} copy(f32[1024,128]{1,0:T(8,128)} %get-tuple-element.28) | data formatting | bytes 1048576
  119.1 1.5 %copy.25 = f32[128,128]{1,0:T(8,128)} copy(f32[128,128]{1,0:T(8,128)} %get-tuple-element.29) | data formatting | bytes 131072
  120.6 1.5 %copy.26 = f32[128,128]{1,0:T(8,128)} copy(f32[128,128]{1,0:T(8,128)} %get-tuple-element.30) | data formatting | bytes 131072
  (1 shorter events, 0.0 us)
Async XLA Ops:
  71.6 44.0 %copy-start.1 = (f32[1024,128]{1,0:T(8,128)S(1)}, f32[1024,128]{1,0:T(8,128)}, u32[]{:S(2)}) copy-start(f32[1024,128]{1,0:T(8,128)} %get-tuple-element.26) | copy-start | bytes 1572868
  71.6 44.8 %copy-start = (f32[1024,128]{1,0:T(8,128)S(1)}, f32[1024,128]{1,0:T(8,128)}, u32[]{:S(2)}) copy-start(f32[1024,128]{1,0:T(8,128)} %get-tuple-element.27) | copy-start | bytes 1572868
